TPU v7x, 512 devices: a whole 4x4x16 slice. The times are simulated.
512 devices in a mesh: ctx: 64 (over z, y), dp: 8 (over x, core).
Axes of the slice: x: 4, y: 4, z: 16, core: 2. Of those that a mesh axis runs over, the one named last changes fastest.
Arguments:
- q_in: bfloat16 [8, 8192, 2048], P('dp', 'ctx'), may hold values from -6 to 6
- k_in: bfloat16 [8, 8192, 2048], P('dp', 'ctx'), may hold values from -6 to 6
- v_in: bfloat16 [8, 8192, 2048], P('dp', 'ctx'), may hold values from -6 to 6
- grad_out: bfloat16 [8, 8192, 2048], P('dp', 'ctx'), may hold values from -6 to 6
- short_filter: float32 [3, 3, 2048], replicated, may hold values from -3.5 to 3.5
- residue: float32 [2048, 8], replicated, may hold values from -2 to 2
- rate: float32 [8], replicated, may hold values from 0.00012207031 to 0.1
Outputs:
- mixed: bfloat16 [8, 8192, 2048], P('dp', 'ctx')
- grad_q: bfloat16 [8, 8192, 2048], P('dp', 'ctx')
- grad_k: bfloat16 [8, 8192, 2048], P('dp', 'ctx')
- grad_v: bfloat16 [8, 8192, 2048], P('dp', 'ctx')
- grad_residue: float32 [2048, 8], P('ctx')
- grad_short: float32 [3, 3, 2048], replicated
All inputs are finite; a program needn't handle non-finite values.
Results may differ from a plain program's by a relative error of at most 0.024.
Values may be sent and summed in bfloat16 or wider, within the bound.
A program may use at most 64 MiB of HBM per device.

v0:
```python
import jax
import jax.numpy as jnp
from jax import lax
from jax.sharding import PartitionSpec as P

BLOCK = 128
PRECISE = lax.Precision.HIGHEST


def passed_along(block, axis, distance):
    devices = range(lax.axis_size(axis))
    route = [(i - distance, i) for i in devices if i - distance in devices]
    return lax.ppermute(block, axis, route)


def mode_sweeps(source, cotangent, rates, columns, gains, front, behind):
    block_len = BLOCK
    block_count = source.shape[1]
    places = jnp.arange(block_len, dtype=jnp.float32)
    offset = places[:, None] - places[None, :]
    blocks = jnp.arange(block_count, dtype=jnp.float32)
    spacing = blocks[:, None] - blocks[None, :] - 1.0
    cot_f = cotangent.astype(jnp.float32)

    def one_mode(carry, item):
        conv_acc, back_acc = carry
        speed, column, start_fwd, start_back = item
        kernel = jnp.where(offset >= 0, jnp.exp(-speed * jnp.maximum(offset, 0.0)), 0.0).astype(
            jnp.bfloat16
        )
        passing = jnp.where(
            spacing >= 0, jnp.exp(-speed * block_len * jnp.maximum(spacing, 0.0)), 0.0
        )
        lead = jnp.exp(-speed * block_len * blocks)
        trail = jnp.exp(-speed * block_len * (block_count - 1.0 - blocks))
        scale_fwd = jnp.exp(-speed * (places + 1.0))
        scale_back = jnp.exp(-speed * (block_len - places))
        inside = jnp.einsum("ts,cns->cnt", kernel, source, preferred_element_type=jnp.float32)
        entering = (
            jnp.einsum("nk,ck->cn", passing, inside[..., block_len - 1], precision=PRECISE)
            + lead[None, :] * start_fwd[:, None]
        )
        forward = inside + scale_fwd[None, None, :] * entering[..., None]
        conv_acc = conv_acc + column[:, None, None] * forward
        grad_row = jnp.sum(forward * cot_f, axis=(1, 2))
        inside_back = jnp.einsum(
            "ts,cnt->cns", kernel, cotangent, preferred_element_type=jnp.float32
        )
        entering_back = (
            jnp.einsum("kn,ck->cn", passing, inside_back[..., 0], precision=PRECISE)
            + trail[None, :] * start_back[:, None]
        )
        backward = inside_back + scale_back[None, None, :] * entering_back[..., None]
        back_acc = back_acc + column[:, None, None] * backward
        return ((conv_acc, back_acc), grad_row)

    zeros_acc = jnp.zeros(source.shape, jnp.float32)
    (conv_sum, back_sum), grads = lax.scan(
        one_mode, (zeros_acc, zeros_acc), (rates, columns, front, behind)
    )
    grads = gains[:, None] * grads
    return (conv_sum, back_sum, grads.T)


def shards(q_in, k_in, v_in, grad_out, short_filter, residue, rate):
    row_count = q_in.shape[1]
    width = q_in.shape[2]
    inputs = (q_in[0], k_in[0], v_in[0])
    tails = jnp.stack([item[row_count - 2 :] for item in inputs])
    before = passed_along(tails, "ctx", 1)
    extended = [
        jnp.concatenate([before[branch], inputs[branch]], axis=0).astype(jnp.float32)
        for branch in range(3)
    ]
    shorts = []
    for branch in range(3):
        total = short_filter[branch, 0][None, :] * extended[branch][2 : 2 + row_count]
        for tap_at in range(1, 3):
            total = (
                total
                + short_filter[branch, tap_at][None, :]
                * extended[branch][2 - tap_at : 2 - tap_at + row_count]
            )
        shorts.append(total)
    query, keyed, valued = shorts
    gated = (keyed * valued).astype(jnp.bfloat16)
    cot_out = grad_out[0].astype(jnp.float32)
    d_conv = (cot_out * query).astype(jnp.bfloat16)
    gains = jnp.sqrt(1.0 - jnp.exp(-2.0 * rate))
    weights = residue * gains[None, :]
    modes = rate.shape[0]
    ctx_count = lax.axis_size("ctx")
    channel_share = width // ctx_count
    owned, incoming = (
        lax.all_to_all(gated, "ctx", split_axis=1, concat_axis=0, tiled=True),
        lax.all_to_all(d_conv, "ctx", split_axis=1, concat_axis=0, tiled=True),
    )
    total_rows = owned.shape[0]
    block_count = total_rows // BLOCK
    owned_lanes = owned.T.reshape(channel_share, block_count, BLOCK)
    incoming_lanes = incoming.T.reshape(channel_share, block_count, BLOCK)
    columns = lax.dynamic_slice_in_dim(
        weights, lax.axis_index("ctx") * channel_share, channel_share, 0
    ).T
    zero_start = jnp.zeros((modes, channel_share), jnp.float32)
    conv_sum, back_sum, partial_value = mode_sweeps(
        owned_lanes, incoming_lanes, rate, columns, gains, zero_start, zero_start
    )
    conv_rows = conv_sum.reshape(channel_share, total_rows).T.astype(jnp.bfloat16)
    back_rows = back_sum.reshape(channel_share, total_rows).T.astype(jnp.bfloat16)
    conv, d_gated = (
        lax.all_to_all(conv_rows, "ctx", split_axis=0, concat_axis=1, tiled=True),
        lax.all_to_all(back_rows, "ctx", split_axis=0, concat_axis=1, tiled=True),
    )
    grad_residue = lax.psum(partial_value, "dp")
    conv_f = conv.astype(jnp.float32)
    mixed = (query * conv_f).astype(jnp.bfloat16)
    gated_back = d_gated.astype(jnp.float32)
    d_shorts = (cot_out * conv_f, gated_back * valued, gated_back * keyed)
    heads = jnp.stack([item[:2] for item in d_shorts])
    after = passed_along(heads.astype(jnp.bfloat16), "ctx", -1).astype(heads.dtype)
    grads = []
    partial_short = []
    for branch in range(3):
        ahead_rows = jnp.concatenate([d_shorts[branch], after[branch]], axis=0)
        total = short_filter[branch, 0][None, :] * ahead_rows[0:row_count]
        for tap_at in range(1, 3):
            total = (
                total
                + short_filter[branch, tap_at][None, :] * ahead_rows[tap_at : tap_at + row_count]
            )
        grads.append(total.astype(jnp.bfloat16)[None])
        partial_short.append(
            jnp.stack(
                [
                    jnp.sum(
                        d_shorts[branch] * extended[branch][2 - tap_at : 2 - tap_at + row_count],
                        axis=0,
                    )
                    for tap_at in range(3)
                ]
            )
        )
    grad_short = lax.psum(jnp.stack(partial_short), ("ctx", "dp"))
    return (mixed[None], grads[0], grads[1], grads[2], grad_residue, grad_short)


def solution(mesh):
    placed = (
        P("dp", "ctx", None),
        P("dp", "ctx", None),
        P("dp", "ctx", None),
        P("dp", "ctx", None),
        P(),
        P(),
        P(),
    )
    return jax.shard_map(
        shards,
        mesh=mesh,
        in_specs=placed,
        out_specs=(
            P("dp", "ctx", None),
            P("dp", "ctx", None),
            P("dp", "ctx", None),
            P("dp", "ctx", None),
            P("ctx", None),
            P(),
        ),
        check_vma=False,
    )
```

profile of v0, /device:TPU:1, one launch (start us, length us, event | category | flops | bytes accessed | tf_op | source)
XLA Modules:
  0.0 703.1 jit_solution(16576350189797462453)
XLA Ops:
  9.5 4.0 collective-permute-start
  18.7 4.5 multiply_convert_fusion
  23.2 18.3 %all-to-all-start = ((bf16[128,64,32]{0,2,1:T(8,128)(2,1)}), bf16[128,64,32]{0,2,1:T(8,128)(2,1)S(1)}, u32[]{:S(2)}, u32[]{:S(2)}) async-start(bf16[128,64,32]{0,2,1:T(8,128)(2,1)} %bitcast.16), calls=%async_computation | async-start | bytes 1048576 | tf_op jit(solution)/shard_map/all_to_all | solution.py:95
  44.2 2.4 fusion.51
  46.6 24.2 %all-to-all-done = bf16[128,64,32]{0,2,1:T(8,128)(2,1)S(1)} async-done(((bf16[128,64,32]{0,2,1:T(8,128)(2,1)}), bf16[128,64,32]{0,2,1:T(8,128)(2,1)S(1)}, u32[]{:S(2)}, u32[]{:S(2)}) %all-to-all-start) | async-done | bytes 524320 | tf_op jit(solution)/shard_map/all_to_all | solution.py:95
  70.7 8.6 %all-to-all-start.1 = ((bf16[128,64,32]{0,2,1:T(8,128)(2,1)}), bf16[128,64,32]{0,2,1:T(8,128)(2,1)S(1)}, u32[]{:S(2)}, u32[]{:S(2)}) async-start(bf16[128,64,32]{0,2,1:T(8,128)(2,1)} %bitcast.20), calls=%async_computation.1 | async-start | bytes 1048576 | tf_op jit(solution)/shard_map/all_to_all | solution.py:96
  81.2 27.1 %all-to-all-done.1 = bf16[128,64,32]{0,2,1:T(8,128)(2,1)S(1)} async-done(((bf16[128,64,32]{0,2,1:T(8,128)(2,1)}), bf16[128,64,32]{0,2,1:T(8,128)(2,1)S(1)}, u32[]{:S(2)}, u32[]{:S(2)}) %all-to-all-start.1) | async-done | bytes 524320 | tf_op jit(solution)/shard_map/all_to_all | solution.py:96
  110.5 60.8 %while.16 = (s32[]{:T(128)}, f32[32,64,128]{2,1,0:T(8,128)}, f32[32,64,128]{2,1,0:T(8,128)}, f32[8,32]{1,0:T(8,128)S(1)}, f32[8,32]{1,0:T(8,128)S(1)}, /*index=5...) while((s32[]{:T(128)}, f32[32,64,128]{2,1,0:T(8,128)}, ...), condition=%wide.region_2.3_spmd.clone.clone, body=%wide.region_0.2_spmd.clone.clone.sunk | while | flops 140759840 | bytes 12668891 | solution.py:58
  114.9 2.2 multiply_reduce_fusion.11
  121.5 3.3 multiply_reduce_fusion.11
  129.2 3.3 multiply_reduce_fusion.11
  133.8 1.4 convolution_bitcast_fusion.5
  137.0 3.3 multiply_reduce_fusion.11
  144.7 3.3 multiply_reduce_fusion.11
  152.5 3.3 multiply_reduce_fusion.11
  157.1 1.4 convolution_bitcast_fusion.5
  160.2 3.3 multiply_reduce_fusion.11
  164.8 1.4 convolution_bitcast_fusion.5
  167.9 3.3 multiply_reduce_fusion.11
  173.8 9.2 %all-to-all-start.3 = ((bf16[64,128,32]{1,2,0:T(8,128)(2,1)}), bf16[64,128,32]{1,2,0:T(8,128)(2,1)}, u32[]{:S(2)}, u32[]{:S(2)}) async-start(bf16[64,128,32]{1,2,0:T(8,128)(2,1)} %copy_bitcast_fusion), calls=%async_computation.3 | async-start | bytes 1048576 | tf_op jit(solution)/shard_map/all_to_all | solution.py:113
  184.3 27.9 %all-to-all-done.3 = bf16[64,128,32]{1,2,0:T(8,128)(2,1)} async-done(((bf16[64,128,32]{1,2,0:T(8,128)(2,1)}), bf16[64,128,32]{1,2,0:T(8,128)(2,1)}, u32[]{:S(2)}, u32[]{:S(2)}) %all-to-all-start.3) | async-done | bytes 524320 | tf_op jit(solution)/shard_map/all_to_all | solution.py:113
  212.1 8.9 %all-to-all-start.2 = ((bf16[64,128,32]{1,2,0:T(8,128)(2,1)}), bf16[64,128,32]{1,2,0:T(8,128)(2,1)}, u32[]{:S(2)}, u32[]{:S(2)}) async-start(bf16[64,128,32]{1,2,0:T(8,128)(2,1)} %copy_bitcast_fusion.1), calls=%async_computation.2 | async-start | bytes 1048576 | tf_op jit(solution)/shard_map/all_to_all | solution.py:112
  221.2 14.6 %psum.14 = f32[32,8]{0,1:T(8,128)} all-reduce(f32[32,8]{0,1:T(8,128)S(1)} %multiply_bitcast_fusion), channel_id=1, replica_groups=mesh['ctx'=64,'dp'=8] {'dp'}, use_global_device_ids=true, to_apply=%region_3.4 | all-reduce | flops 256 | bytes 2048 | tf_op jit(solution)/shard_map/psum | solution.py:115
  235.8 6.3 multiply_reduce_fusion.6
  247.3 2.9 all-to-all-done.2
  250.2 3.0 multiply_reduce_fusion.9
  256.6 1.5 collective-permute-done.1
  260.4 2.2 fusion.76
  262.6 2.2 fusion.75
  264.8 2.2 fusion.74
  270.0 424.7 %all-reduce.2.cloned.1.call-done = f32[3,3,2048]{2,1,0:T(4,128)} async-done(((f32[3,3,2048]{2,1,0:T(4,128)}), f32[3,3,2048]{2,1,0:T(4,128)}) %all-reduce.2.cloned.1.call-update) | async-done | bytes 73744 | tf_op jit(solution)/shard_map/psum | solution.py:144
  694.7 1.5 copy.80
  (183 shorter events, 57.1 us)
Async XLA Ops:
  9.5 7.7 %collective-permute-start = (bf16[3,2,2048]{2,1,0:T(2,128)(2,1)S(1)}, bf16[3,2,2048]{2,1,0:T(2,128)(2,1)S(1)}, u32[]{:S(2)}, u32[]{:S(2)}) collective-permute-start(bf16[3,2,2048]{2,1,0:T(2,128)(2,1)S(1)} %pad_maximum_fusion.4), channel_id=1, source_target_pairs={{0,8},{8,16},{16,24},{24,32},{32,40},{40,48},{48,56},{56,64},{64,7... | collective-permute-start | bytes 73736 | tf_op jit(solution)/shard_map/ppermute | solution.py:13
  18.7 4.5 copy-start.1
  18.7 4.5 copy-start.3
  18.7 22.8 %copy-start.13 = (bf16[1,128,2048]{2,1,0:T(8,128)(2,1)S(1)}, bf16[1,128,2048]{2,1,0:T(8,128)(2,1)}, u32[]{:S(2)}) copy-start(bf16[1,128,2048]{2,1,0:T(8,128)(2,1)} %param.9) | copy-start | bytes 1572868
  23.2 18.6 %copy-start.14 = (bf16[1,128,2048]{2,1,0:T(8,128)(2,1)S(1)}, bf16[1,128,2048]{2,1,0:T(8,128)(2,1)}, u32[]{:S(2)}) copy-start(bf16[1,128,2048]{2,1,0:T(8,128)(2,1)} %param.12) | copy-start | bytes 1572868
  23.2 47.5 %all-to-all-start = ((bf16[128,64,32]{0,2,1:T(8,128)(2,1)}), bf16[128,64,32]{0,2,1:T(8,128)(2,1)S(1)}, u32[]{:S(2)}, u32[]{:S(2)}) async-start(bf16[128,64,32]{0,2,1:T(8,128)(2,1)} %bitcast.16), calls=%async_computation | async-start | bytes 1048576 | tf_op jit(solution)/shard_map/all_to_all | solution.py:95
  42.1 4.5 copy-start.11
  42.8 1.4 copy-start.4
  44.2 35.2 %copy-start.15 = (f32[8]{0:T(128)S(1)}, f32[8]{0:T(128)}, u32[]{:S(2)}) copy-start(f32[8]{0:T(128)} %param.15) | copy-start | bytes 100
  70.7 37.6 %all-to-all-start.1 = ((bf16[128,64,32]{0,2,1:T(8,128)(2,1)}), bf16[128,64,32]{0,2,1:T(8,128)(2,1)S(1)}, u32[]{:S(2)}, u32[]{:S(2)}) async-start(bf16[128,64,32]{0,2,1:T(8,128)(2,1)} %bitcast.20), calls=%async_computation.1 | async-start | bytes 1048576 | tf_op jit(solution)/shard_map/all_to_all | solution.py:96
  111.7 2.0 copy-start.6
  118.3 2.0 copy-start.6
  126.1 2.0 copy-start.6
  133.8 2.0 copy-start.6
  141.6 2.0 copy-start.6
  149.3 2.0 copy-start.6
  157.0 2.0 copy-start.6
  164.8 2.0 copy-start.6
  171.3 11.8 %copy-start = (f32[32,64,128]{2,1,0:T(8,128)S(1)}, f32[32,64,128]{2,1,0:T(8,128)}, u32[]{:S(2)}) copy-start(f32[32,64,128]{2,1,0:T(8,128)} %get-tuple-element.87) | copy-start | bytes 3145732
  173.8 38.3 %all-to-all-start.3 = ((bf16[64,128,32]{1,2,0:T(8,128)(2,1)}), bf16[64,128,32]{1,2,0:T(8,128)(2,1)}, u32[]{:S(2)}, u32[]{:S(2)}) async-start(bf16[64,128,32]{1,2,0:T(8,128)(2,1)} %copy_bitcast_fusion), calls=%async_computation.3 | async-start | bytes 1048576 | tf_op jit(solution)/shard_map/all_to_all | solution.py:113
  183.0 52.7 %copy-start.2 = (f32[130,2048]{0,1:T(8,128)S(1)}, f32[130,2048]{0,1:T(8,128)}, u32[]{:S(2)}) copy-start(f32[130,2048]{0,1:T(8,128)} %copy-done.1) | copy-start | bytes 3194884
  212.1 38.0 %all-to-all-start.2 = ((bf16[64,128,32]{1,2,0:T(8,128)(2,1)}), bf16[64,128,32]{1,2,0:T(8,128)(2,1)}, u32[]{:S(2)}, u32[]{:S(2)}) async-start(bf16[64,128,32]{1,2,0:T(8,128)(2,1)} %copy_bitcast_fusion.1), calls=%async_computation.2 | async-start | bytes 1048576 | tf_op jit(solution)/shard_map/all_to_all | solution.py:112
  221.0 473.7 %all-reduce.2.cloned.1.call-start = ((), (), s32[]{:S(2)}) async-start(), calls=%async_computation.4 | async-start | bytes 196608 | tf_op jit(solution)/shard_map/psum | solution.py:144
  242.1 1.0 copy-start.7
  242.1 8.1 %copy-start.9 = (f32[128,2048]{0,1:T(8,128)}, f32[128,2048]{0,1:T(8,128)S(1)}, u32[]{:S(2)}) copy-start(f32[128,2048]{0,1:T(8,128)S(1)} %get-tuple-element.228) | copy-start | bytes 3145732
  242.1 8.0 %copy-start.5 = (f32[130,2048]{0,1:T(8,128)S(1)}, f32[130,2048]{0,1:T(8,128)}, u32[]{:S(2)}) copy-start(f32[130,2048]{0,1:T(8,128)} %copy-done.4) | copy-start | bytes 3194884
  253.2 2.4 copy-start.12
  253.5 4.6 collective-permute-start.1
  259.1 1.2 copy-start.10
  259.4 3.2 copy-start.8
Sparse Core Ops, SparseCore 0:
  255.7 438.9 all-reduce.1
where the time goes:
time: 705 us; the launch traced here: 703 us
  waiting for transfers between devices  508 us (72%)
  other arithmetic  54 us (8%)
  starting transfers between devices  50.4 us (7%)
  local copies, waits for them, and re-layouts  39.1 us (6%)
  matrix products  16.5 us (2%)
  blocking collectives  14.6 us (2%)
  between operations  14.5 us (2%)
    psum x1, waiting for transfers between devices, shards(): grad_short = lax.psum(jnp.stack(partial_short), ('ctx', 'dp'))  425 us
    all_to_all x1, waiting for transfers between devices, shards(): lax.all_to_all(back_rows, 'ctx', split_axis=0, concat_axis=1, tiled=True)  27.9 us
    all_to_all x1, waiting for transfers between devices, shards(): lax.all_to_all(d_conv, 'ctx', split_axis=1, concat_axis=0, tiled=True)  27.1 us
    reduce_sum x8, other arithmetic, one_mode(): grad_row = jnp.sum(forward * cot_f, axis=(1, 2))  25.3 us
    all_to_all x1, waiting for transfers between devices, shards(): lax.all_to_all(gated, 'ctx', split_axis=1, concat_axis=0, tiled=True)  24.2 us
    all_to_all x1, starting transfers between devices, shards(): lax.all_to_all(gated, 'ctx', split_axis=1, concat_axis=0, tiled=True)  18.3 us
    unnamed x46, local copies, waits for them, and re-layouts  15 us
    psum x1, blocking collectives, shards(): grad_residue = lax.psum(partial_value, 'dp')  14.6 us
  transfers between devices with their start and end apart: 7, of which 6 were waited for; matrix products, arithmetic and copies ran while one was open for 5% of the time, Pallas kernels for 0%

commit v1 on v0

--- a/solution.py
+++ b/solution.py
@@ -141,7 +141,7 @@
                 ]
             )
         )
-    grad_short = lax.psum(jnp.stack(partial_short), ("ctx", "dp"))
+    grad_short = lax.psum(lax.psum(jnp.stack(partial_short), "ctx"), "dp")
     return (mixed[None], grads[0], grads[1], grads[2], grad_residue, grad_short)
 
 

time: 705 us -> 592 us (0.84)
  waiting for transfers between devices: 508 us -> 394 us
    psum x1 -> x2, waiting for transfers between devices: 425 us -> 311 us  [shards(): grad_short = lax.psum(lax.psum(jnp.stack(partial_short), 'ctx'), 'dp')]
    unnamed x46 -> x52, local copies, waits for them, and re-layouts: 15 us -> 15.1 us
  transfers between devices with their start and end apart: 7 -> 8, of which waited for: 6 -> 7; matrix products, arithmetic and copies ran while one was open for 5% -> 6% of each run, Pallas kernels for 0% -> 0%
where the time goes in v1:
time: 592 us; the launch traced here: 591 us
  waiting for transfers between devices  394 us (67%)
  other arithmetic  55.6 us (9%)
  starting transfers between devices  50.5 us (9%)
  local copies, waits for them, and re-layouts  39.1 us (7%)
  matrix products  16.5 us (3%)
  blocking collectives  14.6 us (2%)
  between operations  14.5 us (2%)
    psum x2, waiting for transfers between devices, shards(): grad_short = lax.psum(lax.psum(jnp.stack(partial_short), 'ctx'), 'dp')  311 us
    all_to_all x1, waiting for transfers between devices, shards(): lax.all_to_all(back_rows, 'ctx', split_axis=0, concat_axis=1, tiled=True)  27.9 us
    all_to_all x1, waiting for transfers between devices, shards(): lax.all_to_all(d_conv, 'ctx', split_axis=1, concat_axis=0, tiled=True)  27.1 us
    reduce_sum x8, other arithmetic, one_mode(): grad_row = jnp.sum(forward * cot_f, axis=(1, 2))  25.3 us
    all_to_all x1, waiting for transfers between devices, shards(): lax.all_to_all(gated, 'ctx', split_axis=1, concat_axis=0, tiled=True)  24.2 us
    all_to_all x1, starting transfers between devices, shards(): lax.all_to_all(gated, 'ctx', split_axis=1, concat_axis=0, tiled=True)  18.3 us
    unnamed x52, local copies, waits for them, and re-layouts  15.1 us
    psum x1, blocking collectives, shards(): grad_residue = lax.psum(partial_value, 'dp')  14.6 us
  transfers between devices with their start and end apart: 8, of which 7 were waited for; matrix products, arithmetic and copies ran while one was open for 6% of the time, Pallas kernels for 0%

profile of v1, /device:TPU:1, one launch (start us, length us, event | category | flops | bytes accessed | tf_op | source)
XLA Modules:
  0.0 590.8 jit_solution(9653473878698204474)
XLA Ops:
  9.5 4.0 collective-permute-start
  18.7 4.5 multiply_convert_fusion
  23.2 18.3 %all-to-all-start = ((bf16[128,64,32]{0,2,1:T(8,128)(2,1)}), bf16[128,64,32]{0,2,1:T(8,128)(2,1)S(1)}, u32[]{:S(2)}, u32[]{:S(2)}) async-start(bf16[128,64,32]{0,2,1:T(8,128)(2,1)} %bitcast.16), calls=%async_computation | async-start | bytes 1048576 | tf_op jit(solution)/shard_map/all_to_all | solution.py:95
  44.2 2.4 fusion.51
  46.6 24.2 %all-to-all-done = bf16[128,64,32]{0,2,1:T(8,128)(2,1)S(1)} async-done(((bf16[128,64,32]{0,2,1:T(8,128)(2,1)}), bf16[128,64,32]{0,2,1:T(8,128)(2,1)S(1)}, u32[]{:S(2)}, u32[]{:S(2)}) %all-to-all-start) | async-done | bytes 524320 | tf_op jit(solution)/shard_map/all_to_all | solution.py:95
  70.7 8.6 %all-to-all-start.1 = ((bf16[128,64,32]{0,2,1:T(8,128)(2,1)}), bf16[128,64,32]{0,2,1:T(8,128)(2,1)S(1)}, u32[]{:S(2)}, u32[]{:S(2)}) async-start(bf16[128,64,32]{0,2,1:T(8,128)(2,1)} %bitcast.20), calls=%async_computation.1 | async-start | bytes 1048576 | tf_op jit(solution)/shard_map/all_to_all | solution.py:96
  81.2 27.1 %all-to-all-done.1 = bf16[128,64,32]{0,2,1:T(8,128)(2,1)S(1)} async-done(((bf16[128,64,32]{0,2,1:T(8,128)(2,1)}), bf16[128,64,32]{0,2,1:T(8,128)(2,1)S(1)}, u32[]{:S(2)}, u32[]{:S(2)}) %all-to-all-start.1) | async-done | bytes 524320 | tf_op jit(solution)/shard_map/all_to_all | solution.py:96
  110.5 60.8 %while.16 = (s32[]{:T(128)}, f32[32,64,128]{2,1,0:T(8,128)}, f32[32,64,128]{2,1,0:T(8,128)}, f32[8,32]{1,0:T(8,128)S(1)}, f32[8,32]{1,0:T(8,128)S(1)}, /*index=5...) while((s32[]{:T(128)}, f32[32,64,128]{2,1,0:T(8,128)}, ...), condition=%wide.region_2.3_spmd.clone.clone, body=%wide.region_0.2_spmd.clone.clone.sunk | while | flops 140759840 | bytes 12668891 | solution.py:58
  111.8 1.4 convolution_bitcast_fusion.5
  114.9 2.2 multiply_reduce_fusion.11
  121.5 3.3 multiply_reduce_fusion.11
  129.2 3.3 multiply_reduce_fusion.11
  137.0 3.3 multiply_reduce_fusion.11
  141.6 1.4 convolution_bitcast_fusion.5
  144.7 3.3 multiply_reduce_fusion.11
  152.4 3.3 multiply_reduce_fusion.11
  160.2 3.3 multiply_reduce_fusion.11
  167.9 3.3 multiply_reduce_fusion.11
  173.8 9.2 %all-to-all-start.3 = ((bf16[64,128,32]{1,2,0:T(8,128)(2,1)}), bf16[64,128,32]{1,2,0:T(8,128)(2,1)}, u32[]{:S(2)}, u32[]{:S(2)}) async-start(bf16[64,128,32]{1,2,0:T(8,128)(2,1)} %copy_bitcast_fusion), calls=%async_computation.3 | async-start | bytes 1048576 | tf_op jit(solution)/shard_map/all_to_all | solution.py:113
  184.3 27.9 %all-to-all-done.3 = bf16[64,128,32]{1,2,0:T(8,128)(2,1)} async-done(((bf16[64,128,32]{1,2,0:T(8,128)(2,1)}), bf16[64,128,32]{1,2,0:T(8,128)(2,1)}, u32[]{:S(2)}, u32[]{:S(2)}) %all-to-all-start.3) | async-done | bytes 524320 | tf_op jit(solution)/shard_map/all_to_all | solution.py:113
  212.1 8.9 %all-to-all-start.2 = ((bf16[64,128,32]{1,2,0:T(8,128)(2,1)}), bf16[64,128,32]{1,2,0:T(8,128)(2,1)}, u32[]{:S(2)}, u32[]{:S(2)}) async-start(bf16[64,128,32]{1,2,0:T(8,128)(2,1)} %copy_bitcast_fusion.1), calls=%async_computation.2 | async-start | bytes 1048576 | tf_op jit(solution)/shard_map/all_to_all | solution.py:112
  221.2 14.6 %psum.21 = f32[32,8]{0,1:T(8,128)} all-reduce(f32[32,8]{0,1:T(8,128)S(1)} %multiply_bitcast_fusion), channel_id=1, replica_groups=mesh['ctx'=64,'dp'=8] {'dp'}, use_global_device_ids=true, to_apply=%region_3.4 | all-reduce | flops 256 | bytes 2048 | tf_op jit(solution)/shard_map/psum | solution.py:115
  235.8 6.2 %multiply_reduce_fusion.6 = (f32[2048]{0:T(1024)S(1)}, f32[2048]{0:T(1024)S(1)}, f32[2048]{0:T(1024)S(1)}, f32[128,2048]{0,1:T(8,128)S(1)}, f32[2048]{0:T(1024)S...) fusion(f32[130,2048]{0,1:T(8,128)S(1)} %copy-done.2, f32[128,2048]{0,1:T(8,128)} %get-tuple-element.211, ...), kind=kLoop, calls=%fused_computation.106 | loop fusion | flops 3919872 | bytes 11059200 | tf_op jit(solution)/shard_map/reduce_sum | solution.py:136
  247.2 2.9 all-to-all-done.2
  250.1 3.0 multiply_reduce_fusion.9
  256.6 1.4 collective-permute-done.1
  260.4 2.7 fusion.76
  263.1 2.8 fusion.75
  265.9 237.1 %all-reduce.3.cloned.1.call-done = f32[3,3,2048]{2,1,0:T(4,128)} async-done(((f32[3,3,2048]{2,1,0:T(4,128)}), f32[3,3,2048]{2,1,0:T(4,128)}) %all-reduce.3.cloned.1.call-update) | async-done | bytes 73744 | tf_op jit(solution)/shard_map/psum | solution.py:144
  503.0 2.8 fusion.74
  508.8 73.6 %all-reduce.5.cloned.1.call-done = f32[3,3,2048]{2,1,0:T(4,128)} async-done(((f32[3,3,2048]{2,1,0:T(4,128)}), f32[3,3,2048]{2,1,0:T(4,128)}) %all-reduce.5.cloned.1.call-update) | async-done | bytes 73744 | tf_op jit(solution)/shard_map/psum | solution.py:144
  582.4 1.5 copy.81
  (192 shorter events, 58.6 us)
Async XLA Ops:
  9.5 7.7 %collective-permute-start = (bf16[3,2,2048]{2,1,0:T(2,128)(2,1)S(1)}, bf16[3,2,2048]{2,1,0:T(2,128)(2,1)S(1)}, u32[]{:S(2)}, u32[]{:S(2)}) collective-permute-start(bf16[3,2,2048]{2,1,0:T(2,128)(2,1)S(1)} %pad_maximum_fusion.4), channel_id=1, source_target_pairs={{0,8},{8,16},{16,24},{24,32},{32,40},{40,48},{48,56},{56,64},{64,7... | collective-permute-start | bytes 73736 | tf_op jit(solution)/shard_map/ppermute | solution.py:13
  18.7 4.5 copy-start.1
  18.7 4.5 copy-start.3
  18.7 22.8 %copy-start.16 = (bf16[1,128,2048]{2,1,0:T(8,128)(2,1)S(1)}, bf16[1,128,2048]{2,1,0:T(8,128)(2,1)}, u32[]{:S(2)}) copy-start(bf16[1,128,2048]{2,1,0:T(8,128)(2,1)} %param.9) | copy-start | bytes 1572868
  23.2 18.6 %copy-start.17 = (bf16[1,128,2048]{2,1,0:T(8,128)(2,1)S(1)}, bf16[1,128,2048]{2,1,0:T(8,128)(2,1)}, u32[]{:S(2)}) copy-start(bf16[1,128,2048]{2,1,0:T(8,128)(2,1)} %param.12) | copy-start | bytes 1572868
  23.2 47.5 %all-to-all-start = ((bf16[128,64,32]{0,2,1:T(8,128)(2,1)}), bf16[128,64,32]{0,2,1:T(8,128)(2,1)S(1)}, u32[]{:S(2)}, u32[]{:S(2)}) async-start(bf16[128,64,32]{0,2,1:T(8,128)(2,1)} %bitcast.16), calls=%async_computation | async-start | bytes 1048576 | tf_op jit(solution)/shard_map/all_to_all | solution.py:95
  42.1 4.5 copy-start.11
  42.9 1.3 copy-start.4
  44.2 35.2 %copy-start.18 = (f32[8]{0:T(128)S(1)}, f32[8]{0:T(128)}, u32[]{:S(2)}) copy-start(f32[8]{0:T(128)} %param.15) | copy-start | bytes 100
  70.7 37.6 %all-to-all-start.1 = ((bf16[128,64,32]{0,2,1:T(8,128)(2,1)}), bf16[128,64,32]{0,2,1:T(8,128)(2,1)S(1)}, u32[]{:S(2)}, u32[]{:S(2)}) async-start(bf16[128,64,32]{0,2,1:T(8,128)(2,1)} %bitcast.20), calls=%async_computation.1 | async-start | bytes 1048576 | tf_op jit(solution)/shard_map/all_to_all | solution.py:96
  111.7 2.0 copy-start.6
  118.3 2.0 copy-start.6
  126.1 2.0 copy-start.6
  133.8 2.0 copy-start.6
  141.5 2.0 copy-start.6
  149.3 2.0 copy-start.6
  157.0 2.0 copy-start.6
  164.8 2.0 copy-start.6
  171.3 11.8 %copy-start = (f32[32,64,128]{2,1,0:T(8,128)S(1)}, f32[32,64,128]{2,1,0:T(8,128)}, u32[]{:S(2)}) copy-start(f32[32,64,128]{2,1,0:T(8,128)} %get-tuple-element.87) | copy-start | bytes 3145732
  173.8 38.3 %all-to-all-start.3 = ((bf16[64,128,32]{1,2,0:T(8,128)(2,1)}), bf16[64,128,32]{1,2,0:T(8,128)(2,1)}, u32[]{:S(2)}, u32[]{:S(2)}) async-start(bf16[64,128,32]{1,2,0:T(8,128)(2,1)} %copy_bitcast_fusion), calls=%async_computation.3 | async-start | bytes 1048576 | tf_op jit(solution)/shard_map/all_to_all | solution.py:113
  183.0 52.7 %copy-start.2 = (f32[130,2048]{0,1:T(8,128)S(1)}, f32[130,2048]{0,1:T(8,128)}, u32[]{:S(2)}) copy-start(f32[130,2048]{0,1:T(8,128)} %copy-done.1) | copy-start | bytes 3194884
  212.1 38.0 %all-to-all-start.2 = ((bf16[64,128,32]{1,2,0:T(8,128)(2,1)}), bf16[64,128,32]{1,2,0:T(8,128)(2,1)}, u32[]{:S(2)}, u32[]{:S(2)}) async-start(bf16[64,128,32]{1,2,0:T(8,128)(2,1)} %copy_bitcast_fusion.1), calls=%async_computation.2 | async-start | bytes 1048576 | tf_op jit(solution)/shard_map/all_to_all | solution.py:112
  221.0 281.9 %all-reduce.3.cloned.1.call-start = ((), (), s32[]{:S(2)}) async-start(), calls=%async_computation.4 | async-start | bytes 196608 | tf_op jit(solution)/shard_map/psum | solution.py:144
  242.0 8.1 %copy-start.9 = (f32[128,2048]{0,1:T(8,128)}, f32[128,2048]{0,1:T(8,128)S(1)}, u32[]{:S(2)}) copy-start(f32[128,2048]{0,1:T(8,128)S(1)} %get-tuple-element.228) | copy-start | bytes 3145732
  242.0 8.1 %copy-start.5 = (f32[130,2048]{0,1:T(8,128)S(1)}, f32[130,2048]{0,1:T(8,128)}, u32[]{:S(2)}) copy-start(f32[130,2048]{0,1:T(8,128)} %copy-done.4) | copy-start | bytes 3194884
  253.1 2.5 copy-start.15
  253.5 4.6 collective-permute-start.1
  255.6 326.8 %all-reduce.5.cloned.1.call-start = ((), (), s32[]{:S(2)}) async-start(), calls=%async_computation.5 | async-start | bytes 196608 | tf_op jit(solution)/shard_map/psum | solution.py:144
  259.4 3.8 copy-start.8
  265.9 239.9 %copy-start.12 = (bf16[1,128,2048]{1,2,0:T(8,128)(2,1)S(1)}, bf16[1,128,2048]{1,2,0:T(8,128)(2,1)}, u32[]{:S(2)}) copy-start(bf16[1,128,2048]{1,2,0:T(8,128)(2,1)} %fusion.76) | copy-start | bytes 1572868
  265.9 240.9 %copy-start.13 = (bf16[1,128,2048]{1,2,0:T(8,128)(2,1)S(1)}, bf16[1,128,2048]{1,2,0:T(8,128)(2,1)}, u32[]{:S(2)}) copy-start(bf16[1,128,2048]{1,2,0:T(8,128)(2,1)} %fusion.75) | copy-start | bytes 1572868
  505.8 2.0 copy-start.14
  (2 other events, 2.2 us)
Sparse Core Ops, SparseCore 0:
  255.7 247.2 all-reduce.2
  505.3 77.0 all-reduce.4
